TPU v7x, 32 devices: a whole 2x2x4 slice. The times are simulated.
32 devices in a mesh: span: 2 (over y), tmpl: 2 (over x), stn: 8 (over z, core).
Axes of the slice: x: 2, y: 2, z: 4, core: 2. Of those that a mesh axis runs over, the one named last changes fastest.
Arguments:
- signal: bfloat16 [3072, 8192], P('stn', ('span', 'tmpl')), parts along dimension 1, may hold values from -110 to 110
- waveforms: bfloat16 [16, 4, 8, 300], P('tmpl'), may hold values from -40 to 40
- station_groups: int32 [16, 4], P('tmpl'), may hold values from 0 to 7, all different within a row; in each aligned block of 8 rows (0 to 7, 8 to 15, ...) at most 8 rows name the same one
- channel_offsets: int32 [16, 4, 8], P('tmpl'), may hold values from 0 to 383
- moveouts: int32 [16, 4, 8], P('tmpl'), may hold values from 0 to 639
Outputs:
- stack: float32 [16, 6144], P(('tmpl', 'stn'), 'span'), parts along dimension 1
There are 2 independent parts, one for each index of `span`. A program takes and returns all parts, laid end to end along the dimension named above; an argument that names none is the same for every part. Nothing has to cross between parts.
Inputs may be any that keep to these rules, and one draw needn't show every extreme that they name: `station_groups`: A template's 4 station groups are distinct. Among the 8 templates of one index of tmpl, at most 8 touch any one station group, and in every draw some station group is touched by exactly 8 of them.
All inputs are finite; a program needn't handle non-finite values.
Results may differ from a plain program's by a relative error of at most 0.0003.
Values may be sent and summed in bfloat16 or wider, within the bound.
No kernel may reach another device: no remote copies, remote signals or barrier semaphores. Data moves between devices by JAX's collectives and lax.ppermute only.
A program may use at most 64 MiB of HBM per device.

v0:
```python
import jax
import jax.numpy as jnp
from jax import lax
from jax.sharding import PartitionSpec as P

L = 300
NT = 3072
eps_value = 1e-05


def toeplitz_tiles(wave):
    length = wave.shape[0]
    padded = jnp.concatenate(
        [jnp.zeros((128,), wave.dtype), wave, jnp.zeros((513 - length,), wave.dtype)]
    )
    repeated = jnp.tile(padded, 128)[: 128 * 640].reshape(128, 640)
    return repeated[:, 128:640]


def entry_stack(wave_rows, chan_rows, move_rows, series, rms_data):
    toeplitz = jax.vmap(toeplitz_tiles)(wave_rows)
    blocks = NT // 128

    def one_slot(channel, lag_shift):
        data_row = lax.dynamic_slice(series, (channel, lag_shift), (1, NT + 384))
        energy = lax.dynamic_slice(rms_data, (channel, lag_shift), (1, NT))
        return (data_row.reshape(blocks + 3, 128), energy.reshape(NT))

    segments, scales = jax.vmap(one_slot)(chan_rows, move_rows)
    correl = jnp.zeros((wave_rows.shape[0], blocks, 128), jnp.float32)
    for offset in range(4):
        correl = correl + jnp.einsum(
            "pac,pbc->pab",
            segments[:, offset : offset + blocks],
            toeplitz[:, :, offset * 128 : (offset + 1) * 128],
            preferred_element_type=jnp.float32,
        )
    waves_wide = wave_rows.astype(jnp.float32)
    wave_rms = jnp.sqrt(jnp.mean(waves_wide * waves_wide, axis=1) + eps_value)
    normed = correl.reshape(wave_rows.shape[0], NT) / (L * wave_rms[:, None] * scales)
    return jnp.sum(normed, axis=0)


def add_sources(received):
    return jnp.sum(received, axis=0)


def shards(signal, waveforms, station_groups, channel_offsets, moveouts):
    series = lax.all_gather(signal, "tmpl", axis=1, tiled=True)
    group_rows = waveforms.shape[0]
    touch_count = station_groups.shape[1]
    station_count = lax.axis_size("stn")
    own_rows = group_rows // station_count
    capacity = min(group_rows, 2 * group_rows * touch_count // station_count)
    station = lax.axis_index("stn")
    is_local = station_groups == station
    present = jnp.any(is_local, axis=1)
    touch_pick = jnp.sum(
        is_local.astype(jnp.int32) * jnp.arange(touch_count, dtype=jnp.int32)[None, :], axis=1
    )
    position = jnp.cumsum(present.astype(jnp.int32)) - 1
    target = jnp.where(present, position, capacity)
    entry_tpl = (
        jnp.zeros((capacity,), jnp.int32)
        .at[target]
        .set(jnp.arange(group_rows, dtype=jnp.int32), mode="drop")
    )
    entry_touch = touch_pick[entry_tpl]
    live_count = jnp.sum(present.astype(jnp.int32))
    is_live = jnp.arange(capacity, dtype=jnp.int32) < live_count
    wave_sel = waveforms[entry_tpl, entry_touch]
    chan_sel = channel_offsets[entry_tpl, entry_touch]
    move_sel = moveouts[entry_tpl, entry_touch]
    wide_series = series.astype(jnp.float32)
    squares = wide_series * wide_series
    running = jnp.concatenate(
        [jnp.zeros((series.shape[0], 1), jnp.float32), jnp.cumsum(squares, axis=1)], axis=1
    )
    windows = running[:, L:] - running[:, :-L]
    rms_data = jnp.sqrt(windows / L + eps_value)

    def run_entry(entry_num):
        stacked = entry_stack(
            wave_sel[entry_num], chan_sel[entry_num], move_sel[entry_num], series, rms_data
        )
        return jnp.where(is_live[entry_num], stacked, 0.0)

    stacks = lax.map(run_entry, jnp.arange(capacity, dtype=jnp.int32))
    partial_sum = jnp.zeros((group_rows, NT), jnp.float32).at[entry_tpl].add(stacks)
    by_owner = partial_sum.reshape(station_count, own_rows, NT)
    return add_sources(lax.all_to_all(by_owner, "stn", split_axis=0, concat_axis=0, tiled=True))


def solution(mesh):
    in_specs = (
        P("stn", ("span", "tmpl")),
        P("tmpl", None, None, None),
        P("tmpl", None),
        P("tmpl", None, None),
        P("tmpl", None, None),
    )
    out_specs = P(("tmpl", "stn"), "span")
    return jax.shard_map(shards, mesh=mesh, in_specs=in_specs, out_specs=out_specs, check_vma=False)
```

profile of v0, /device:TPU:0, one launch (start us, length us, event | category | flops | bytes accessed | tf_op | source)
XLA Modules:
  0.0 578.0 jit_solution(9084490409785776008)
XLA Ops:
  14.1 42.4 %all-gather.2.cloned.1.call-done = bf16[384,4096]{1,0:T(8,128)(2,1)} async-done(((bf16[384,2048]{1,0:T(8,128)(2,1)}), bf16[384,4096]{1,0:T(8,128)(2,1)}) %all-gather.2.cloned.1.call-update) | async-done | bytes 3145744 | tf_op jit(solution)/shard_map/all_gather | solution.py:49
  56.5 2.6 multiply_bitcast_fusion
  59.2 3.9 copy.30
  63.1 6.7 %copy.20 = f32[384,32,128]{0,1,2:T(8,128)} copy(f32[384,32,128]{2,1,0:T(8,128)} %bitcast.101) | data formatting | bytes 12582912 | tf_op jit(solution)/shard_map/reshape.2
  69.9 3.2 fusion.29
  73.1 2.7 copy-done.1
  75.8 3.5 broadcast_add_fusion
  79.3 3.6 copy.21
  83.0 5.2 fusion.16
  88.1 6.5 %copy.22 = f32[384,3797]{1,0:T(8,128)} copy(f32[384,3797]{0,1:T(8,128)} %fusion.16) | data formatting | bytes 11664384 | tf_op jit(solution)/shard_map/while | solution.py:88
  94.6 464.3 %while.21 = (s32[]{:T(128)}, f32[8,3072]{1,0:T(8,128)S(1)}, s32[8]{0:T(128)S(1)}, pred[8]{0:T(512)(128)(4,1)S(1)}, s32[8,8]{1,0:T(8,128)S(1)}, /*index=5*/s32[8,...) while((s32[]{:T(128)}, f32[8,3072]{1,0:T(8,128)S(1)}, ...), condition=%wide.region_10.11_spmd.clone, body=%wide.region_7.10_spmd.sunk.clone | while | flops 25351368 | bytes 14289844 | solution.py:88
  97.4 24.5 %while.19 = (s32[]{:T(128)}, bf16[384,4096]{1,0:T(8,128)(2,1)}, s32[8,2]{0,1:T(2,128)S(1)}, bf16[8,1,3456]{2,0,1:T(8,128)(2,1)S(1)}, s32[]{:T(128)}, /*index=5*/s32[]{:T(128)}) while((s32[]{:T(128)}, bf16[384,4096]{1,0:T(8,128)(2,1)}, s32[8,2]{0,1:T(2,128)S(1)}, bf16[8,1,3456]{2,0,1:T(8,128)(2,1)S(1)}, s32[]{:T(128)}, /*index=5*/s32[]{:T(128)}) %tuple.81), condition=%wide.while_cond, body=%wide.while_body.sunk | while | flops 2 | bytes 27765 | solution.py:25
  122.3 2.3 reshape.276
  127.1 23.6 %while.20 = (s32[]{:T(128)}, f32[384,3797]{1,0:T(8,128)}, s32[8,2]{0,1:T(2,128)S(1)}, f32[8,1,3072]{2,1,0:T(1,128)S(1)}, s32[]{:T(128)}) while((s32[]{:T(128)}, f32[384,3797]{1,0:T(8,128)}, s32[8,2]{0,1:T(2,128)S(1)}, f32[8,1,3072]{2,1,0:T(1,128)S(1)}, s32[]{:T(128)}) %tuple.84), condition=%wide.while_cond.1, body=%wide.while_body.1.sunk | while | flops 2 | bytes 24685 | solution.py:26
  127.8 2.3 bitcast_dynamic-update-slice_fusion.2
  130.7 2.3 bitcast_dynamic-update-slice_fusion.2
  133.7 2.3 bitcast_dynamic-update-slice_fusion.2
  136.6 2.3 bitcast_dynamic-update-slice_fusion.2
  139.6 2.3 bitcast_dynamic-update-slice_fusion.2
  142.5 2.3 bitcast_dynamic-update-slice_fusion.2
  145.5 2.3 bitcast_dynamic-update-slice_fusion.2
  155.5 24.5 %while.19 = (s32[]{:T(128)}, bf16[384,4096]{1,0:T(8,128)(2,1)}, s32[8,2]{0,1:T(2,128)S(1)}, bf16[8,1,3456]{2,0,1:T(8,128)(2,1)S(1)}, s32[]{:T(128)}, /*index=5*/s32[]{:T(128)}) while((s32[]{:T(128)}, bf16[384,4096]{1,0:T(8,128)(2,1)}, s32[8,2]{0,1:T(2,128)S(1)}, bf16[8,1,3456]{2,0,1:T(8,128)(2,1)S(1)}, s32[]{:T(128)}, /*index=5*/s32[]{:T(128)}) %tuple.81), condition=%wide.while_cond, body=%wide.while_body.sunk | while | flops 2 | bytes 27765 | solution.py:25
  180.4 2.3 reshape.276
  185.1 23.6 %while.20 = (s32[]{:T(128)}, f32[384,3797]{1,0:T(8,128)}, s32[8,2]{0,1:T(2,128)S(1)}, f32[8,1,3072]{2,1,0:T(1,128)S(1)}, s32[]{:T(128)}) while((s32[]{:T(128)}, f32[384,3797]{1,0:T(8,128)}, s32[8,2]{0,1:T(2,128)S(1)}, f32[8,1,3072]{2,1,0:T(1,128)S(1)}, s32[]{:T(128)}) %tuple.84), condition=%wide.while_cond.1, body=%wide.while_body.1.sunk | while | flops 2 | bytes 24685 | solution.py:26
  188.8 2.3 bitcast_dynamic-update-slice_fusion.2
  197.6 2.3 bitcast_dynamic-update-slice_fusion.2
  200.6 2.3 bitcast_dynamic-update-slice_fusion.2
  213.5 24.5 %while.19 = (s32[]{:T(128)}, bf16[384,4096]{1,0:T(8,128)(2,1)}, s32[8,2]{0,1:T(2,128)S(1)}, bf16[8,1,3456]{2,0,1:T(8,128)(2,1)S(1)}, s32[]{:T(128)}, /*index=5*/s32[]{:T(128)}) while((s32[]{:T(128)}, bf16[384,4096]{1,0:T(8,128)(2,1)}, s32[8,2]{0,1:T(2,128)S(1)}, bf16[8,1,3456]{2,0,1:T(8,128)(2,1)S(1)}, s32[]{:T(128)}, /*index=5*/s32[]{:T(128)}) %tuple.81), condition=%wide.while_cond, body=%wide.while_body.sunk | while | flops 2 | bytes 27765 | solution.py:25
  238.4 2.3 reshape.276
  243.2 23.6 %while.20 = (s32[]{:T(128)}, f32[384,3797]{1,0:T(8,128)}, s32[8,2]{0,1:T(2,128)S(1)}, f32[8,1,3072]{2,1,0:T(1,128)S(1)}, s32[]{:T(128)}) while((s32[]{:T(128)}, f32[384,3797]{1,0:T(8,128)}, s32[8,2]{0,1:T(2,128)S(1)}, f32[8,1,3072]{2,1,0:T(1,128)S(1)}, s32[]{:T(128)}) %tuple.84), condition=%wide.while_cond.1, body=%wide.while_body.1.sunk | while | flops 2 | bytes 24685 | solution.py:26
  243.9 2.3 bitcast_dynamic-update-slice_fusion.2
  252.7 2.3 bitcast_dynamic-update-slice_fusion.2
  255.7 2.3 bitcast_dynamic-update-slice_fusion.2
  264.5 2.3 bitcast_dynamic-update-slice_fusion.2
  271.5 24.5 %while.19 = (s32[]{:T(128)}, bf16[384,4096]{1,0:T(8,128)(2,1)}, s32[8,2]{0,1:T(2,128)S(1)}, bf16[8,1,3456]{2,0,1:T(8,128)(2,1)S(1)}, s32[]{:T(128)}, /*index=5*/s32[]{:T(128)}) while((s32[]{:T(128)}, bf16[384,4096]{1,0:T(8,128)(2,1)}, s32[8,2]{0,1:T(2,128)S(1)}, bf16[8,1,3456]{2,0,1:T(8,128)(2,1)S(1)}, s32[]{:T(128)}, /*index=5*/s32[]{:T(128)}) %tuple.81), condition=%wide.while_cond, body=%wide.while_body.sunk | while | flops 2 | bytes 27765 | solution.py:25
  296.5 2.3 reshape.276
  301.2 23.6 %while.20 = (s32[]{:T(128)}, f32[384,3797]{1,0:T(8,128)}, s32[8,2]{0,1:T(2,128)S(1)}, f32[8,1,3072]{2,1,0:T(1,128)S(1)}, s32[]{:T(128)}) while((s32[]{:T(128)}, f32[384,3797]{1,0:T(8,128)}, s32[8,2]{0,1:T(2,128)S(1)}, f32[8,1,3072]{2,1,0:T(1,128)S(1)}, s32[]{:T(128)}) %tuple.84), condition=%wide.while_cond.1, body=%wide.while_body.1.sunk | while | flops 2 | bytes 24685 | solution.py:26
  307.8 2.3 bitcast_dynamic-update-slice_fusion.2
  310.8 2.3 bitcast_dynamic-update-slice_fusion.2
  319.6 2.3 bitcast_dynamic-update-slice_fusion.2
  329.6 24.5 %while.19 = (s32[]{:T(128)}, bf16[384,4096]{1,0:T(8,128)(2,1)}, s32[8,2]{0,1:T(2,128)S(1)}, bf16[8,1,3456]{2,0,1:T(8,128)(2,1)S(1)}, s32[]{:T(128)}, /*index=5*/s32[]{:T(128)}) while((s32[]{:T(128)}, bf16[384,4096]{1,0:T(8,128)(2,1)}, s32[8,2]{0,1:T(2,128)S(1)}, bf16[8,1,3456]{2,0,1:T(8,128)(2,1)S(1)}, s32[]{:T(128)}, /*index=5*/s32[]{:T(128)}) %tuple.81), condition=%wide.while_cond, body=%wide.while_body.sunk | while | flops 2 | bytes 27765 | solution.py:25
  354.5 2.3 reshape.276
  359.3 23.6 %while.20 = (s32[]{:T(128)}, f32[384,3797]{1,0:T(8,128)}, s32[8,2]{0,1:T(2,128)S(1)}, f32[8,1,3072]{2,1,0:T(1,128)S(1)}, s32[]{:T(128)}) while((s32[]{:T(128)}, f32[384,3797]{1,0:T(8,128)}, s32[8,2]{0,1:T(2,128)S(1)}, f32[8,1,3072]{2,1,0:T(1,128)S(1)}, s32[]{:T(128)}) %tuple.84), condition=%wide.while_cond.1, body=%wide.while_body.1.sunk | while | flops 2 | bytes 24685 | solution.py:26
  362.9 2.3 bitcast_dynamic-update-slice_fusion.2
  365.8 2.3 bitcast_dynamic-update-slice_fusion.2
  374.7 2.3 bitcast_dynamic-update-slice_fusion.2
  387.6 24.5 %while.19 = (s32[]{:T(128)}, bf16[384,4096]{1,0:T(8,128)(2,1)}, s32[8,2]{0,1:T(2,128)S(1)}, bf16[8,1,3456]{2,0,1:T(8,128)(2,1)S(1)}, s32[]{:T(128)}, /*index=5*/s32[]{:T(128)}) while((s32[]{:T(128)}, bf16[384,4096]{1,0:T(8,128)(2,1)}, s32[8,2]{0,1:T(2,128)S(1)}, bf16[8,1,3456]{2,0,1:T(8,128)(2,1)S(1)}, s32[]{:T(128)}, /*index=5*/s32[]{:T(128)}) %tuple.81), condition=%wide.while_cond, body=%wide.while_body.sunk | while | flops 2 | bytes 27765 | solution.py:25
  412.6 2.3 reshape.276
  417.3 23.6 %while.20 = (s32[]{:T(128)}, f32[384,3797]{1,0:T(8,128)}, s32[8,2]{0,1:T(2,128)S(1)}, f32[8,1,3072]{2,1,0:T(1,128)S(1)}, s32[]{:T(128)}) while((s32[]{:T(128)}, f32[384,3797]{1,0:T(8,128)}, s32[8,2]{0,1:T(2,128)S(1)}, f32[8,1,3072]{2,1,0:T(1,128)S(1)}, s32[]{:T(128)}) %tuple.84), condition=%wide.while_cond.1, body=%wide.while_body.1.sunk | while | flops 2 | bytes 24685 | solution.py:26
  418.0 2.3 bitcast_dynamic-update-slice_fusion.2
  420.9 2.3 bitcast_dynamic-update-slice_fusion.2
  429.8 2.3 bitcast_dynamic-update-slice_fusion.2
  445.7 24.5 %while.19 = (s32[]{:T(128)}, bf16[384,4096]{1,0:T(8,128)(2,1)}, s32[8,2]{0,1:T(2,128)S(1)}, bf16[8,1,3456]{2,0,1:T(8,128)(2,1)S(1)}, s32[]{:T(128)}, /*index=5*/s32[]{:T(128)}) while((s32[]{:T(128)}, bf16[384,4096]{1,0:T(8,128)(2,1)}, s32[8,2]{0,1:T(2,128)S(1)}, bf16[8,1,3456]{2,0,1:T(8,128)(2,1)S(1)}, s32[]{:T(128)}, /*index=5*/s32[]{:T(128)}) %tuple.81), condition=%wide.while_cond, body=%wide.while_body.sunk | while | flops 2 | bytes 27765 | solution.py:25
  470.6 2.3 reshape.276
  475.3 23.6 %while.20 = (s32[]{:T(128)}, f32[384,3797]{1,0:T(8,128)}, s32[8,2]{0,1:T(2,128)S(1)}, f32[8,1,3072]{2,1,0:T(1,128)S(1)}, s32[]{:T(128)}) while((s32[]{:T(128)}, f32[384,3797]{1,0:T(8,128)}, s32[8,2]{0,1:T(2,128)S(1)}, f32[8,1,3072]{2,1,0:T(1,128)S(1)}, s32[]{:T(128)}) %tuple.84), condition=%wide.while_cond.1, body=%wide.while_body.1.sunk | while | flops 2 | bytes 24685 | solution.py:26
  476.0 2.3 bitcast_dynamic-update-slice_fusion.2
  484.9 2.3 bitcast_dynamic-update-slice_fusion.2
  496.7 2.3 bitcast_dynamic-update-slice_fusion.2
  503.7 24.5 %while.19 = (s32[]{:T(128)}, bf16[384,4096]{1,0:T(8,128)(2,1)}, s32[8,2]{0,1:T(2,128)S(1)}, bf16[8,1,3456]{2,0,1:T(8,128)(2,1)S(1)}, s32[]{:T(128)}, /*index=5*/s32[]{:T(128)}) while((s32[]{:T(128)}, bf16[384,4096]{1,0:T(8,128)(2,1)}, s32[8,2]{0,1:T(2,128)S(1)}, bf16[8,1,3456]{2,0,1:T(8,128)(2,1)S(1)}, s32[]{:T(128)}, /*index=5*/s32[]{:T(128)}) %tuple.81), condition=%wide.while_cond, body=%wide.while_body.sunk | while | flops 2 | bytes 27765 | solution.py:25
  528.6 2.3 reshape.276
  533.4 23.6 %while.20 = (s32[]{:T(128)}, f32[384,3797]{1,0:T(8,128)}, s32[8,2]{0,1:T(2,128)S(1)}, f32[8,1,3072]{2,1,0:T(1,128)S(1)}, s32[]{:T(128)}) while((s32[]{:T(128)}, f32[384,3797]{1,0:T(8,128)}, s32[8,2]{0,1:T(2,128)S(1)}, f32[8,1,3072]{2,1,0:T(1,128)S(1)}, s32[]{:T(128)}) %tuple.84), condition=%wide.while_cond.1, body=%wide.while_body.1.sunk | while | flops 2 | bytes 24685 | solution.py:26
  540.0 2.3 bitcast_dynamic-update-slice_fusion.2
  551.8 2.3 bitcast_dynamic-update-slice_fusion.2
  559.8 10.7 %all_to_all.5 = f32[8,1,3072]{2,1,0:T(1,128)S(1)} all-to-all(f32[8,1,3072]{2,1,0:T(1,128)S(1)} %reshape.180), channel_id=1, replica_groups=mesh['span'=2,'tmpl'=2,'stn'=8] {'stn'}, dimensions={0} | all-to-all | bytes 196608 | tf_op jit(solution)/shard_map/all_to_all | solution.py:91
  (641 shorter events, 371.2 us)
Async XLA Ops:
  6.5 3.0 copy-start
  6.5 50.0 %all-gather.2.cloned.1.call-start = ((), (), s32[]{:S(2)}) async-start(), calls=%async_computation.1 | async-start | bytes 4718592 | tf_op jit(solution)/shard_map/all_gather | solution.py:49
  73.1 2.7 copy-start.1
Sparse Core Ops, SparseCore 0:
  8.9 47.6 all-gather.1
where the time goes:
time: 586 us; the launch traced here: 578 us
  local copies, waits for them, and re-layouts  457 us (78%)
  waiting for transfers between devices  43.2 us (7%)
  other arithmetic  25.2 us (4%)
  loops' own time  20.5 us (3%)
  between operations  13.5 us (2%)
  blocking collectives  10.7 us (2%)
  matrix products  8.11 us (1%)
    gather x448, local copies, waits for them, and re-layouts  382 us
    all_gather x1, waiting for transfers between devices, shards(): series = lax.all_gather(signal, 'tmpl', axis=1, tiled=True)  42.4 us
    while x16, local copies, waits for them, and re-layouts  19.7 us
    another operation x1, loops' own time, shards(): stacks = lax.map(run_entry, jnp.arange(capacity, dtype=jnp.int32))  17.7 us
    another operation x16, local copies, waits for them, and re-layouts, toeplitz_tiles(): repeated = jnp.tile(padded, 128)[:128 * 640].reshape(128, 640)  12.1 us
  transfers between devices with their start and end apart: 1, of which 1 were waited for; matrix products, arithmetic and copies ran while one was open for 1% of the time, Pallas kernels for 0%

commit v1 on v0

--- a/solution.py
+++ b/solution.py
@@ -46,7 +46,15 @@
 
 
 def shards(signal, waveforms, station_groups, channel_offsets, moveouts):
-    series = lax.all_gather(signal, "tmpl", axis=1, tiled=True)
+    ways, here = (lax.axis_size("tmpl"), lax.axis_index("tmpl"))
+    grown, reach = (signal, 1)
+    while reach < ways:
+        theirs = lax.ppermute(grown, "tmpl", [(d, d ^ reach) for d in range(ways)])
+        mine_first = jnp.concatenate([grown, theirs], axis=1)
+        theirs_first = jnp.concatenate([theirs, grown], axis=1)
+        grown = jnp.where(here & reach == 0, mine_first, theirs_first)
+        reach = 2 * reach
+    series = grown
     group_rows = waveforms.shape[0]
     touch_count = station_groups.shape[1]
     station_count = lax.axis_size("stn")

time: 586 us -> 553 us (0.944)
  waiting for transfers between devices: 43.2 us -> 24.4 us
  between operations: 13.5 us -> 0.12 us
  local copies, waits for them, and re-layouts: 457 us -> 451 us
    all_gather x1 -> x0, waiting for transfers between devices: 42.4 us -> none  [shards(): series = lax.all_gather(signal, 'tmpl', axis=1, tiled=True)]
    ppermute x0 -> x1, waiting for transfers between devices: none -> 24.4 us  [shards(): theirs = lax.ppermute(grown, 'tmpl', [(d, d ^ reach) for d in range(ways)])]
    another operation x20 -> x19, local copies, waits for them, and re-layouts: 10.4 us -> 4.5 us
  transfers between devices with their start and end apart: 1 -> 1, of which waited for: 1 -> 1; matrix products, arithmetic and copies ran while one was open for 1% -> 2% of each run, Pallas kernels for 0% -> 0%
where the time goes in v1:
time: 553 us; the launch traced here: 545 us
  local copies, waits for them, and re-layouts  451 us (82%)
  other arithmetic  27.2 us (5%)
  waiting for transfers between devices  24.4 us (4%)
  loops' own time  20.5 us (4%)
  blocking collectives  11.2 us (2%)
  matrix products  8.1 us (1%)
    gather x448, local copies, waits for them, and re-layouts  380 us
    ppermute x1, waiting for transfers between devices, shards(): theirs = lax.ppermute(grown, 'tmpl', [(d, d ^ reach) for d in range(ways)])  24.4 us
    while x16, local copies, waits for them, and re-layouts  19.7 us
    another operation x1, loops' own time, shards(): stacks = lax.map(run_entry, jnp.arange(capacity, dtype=jnp.int32))  17.6 us
    another operation x16, local copies, waits for them, and re-layouts, toeplitz_tiles(): repeated = jnp.tile(padded, 128)[:128 * 640].reshape(128, 640)  12.1 us
    all_to_all x1, blocking collectives, shards(): lax.all_to_all(by_owner, 'stn', split_axis=0, concat_axis=0, tiled=True)  11.2 us
  transfers between devices with their start and end apart: 1, of which 1 were waited for; matrix products, arithmetic and copies ran while one was open for 2% of the time, Pallas kernels for 0%

profile of v1, /device:TPU:0, one launch (start us, length us, event | category | flops | bytes accessed | tf_op | source)
XLA Modules:
  0.0 545.3 jit_solution(13455923340178657508)
XLA Ops:
  0.0 3.0 collective-permute-start
  13.2 24.4 %collective-permute-done = bf16[384,2048]{1,0:T(8,128)(2,1)} collective-permute-done((bf16[384,2048]{1,0:T(8,128)(2,1)}, bf16[384,2048]{1,0:T(8,128)(2,1)}, u32[]{:S(2)}, u32[]{:S(2)}) %collective-permute-start) | collective-permute-done | bytes 1572896 | tf_op jit(solution)/shard_map/ppermute | solution.py:52
  37.7 3.0 copy.40
  40.7 2.6 copy.27
  43.3 3.6 fusion.13
  47.8 3.5 broadcast_add_fusion
  51.2 3.6 copy.30
  54.9 5.2 fusion.19
  60.1 6.6 %copy.31 = f32[384,3797]{1,0:T(8,128)} copy(f32[384,3797]{0,1:T(8,128)} %fusion.19) | data formatting | bytes 11664384 | tf_op jit(solution)/shard_map/while | solution.py:96
  66.7 4.2 maximum_select_fusion
  70.9 461.7 %while.21 = (s32[]{:T(128)}, f32[8,3072]{1,0:T(8,128)S(1)}, s32[8]{0:T(128)S(1)}, pred[8]{0:T(512)(128)(4,1)S(1)}, s32[8,8]{1,0:T(8,128)S(1)}, /*index=5*/s32[8,...) while((s32[]{:T(128)}, f32[8,3072]{1,0:T(8,128)S(1)}, ...), condition=%wide.region_10.11_spmd.clone, body=%wide.region_7.10_spmd.sunk.clone | while | flops 25351368 | bytes 14289844 | solution.py:96
  73.7 24.4 %while.19 = (s32[]{:T(128)}, bf16[384,4096]{1,0:T(8,128)(2,1)}, s32[8,2]{0,1:T(2,128)S(1)}, bf16[8,1,3456]{2,0,1:T(8,128)(2,1)S(1)}, s32[]{:T(128)}, /*index=5*/s32[]{:T(128)}) while((s32[]{:T(128)}, bf16[384,4096]{1,0:T(8,128)(2,1)}, s32[8,2]{0,1:T(2,128)S(1)}, bf16[8,1,3456]{2,0,1:T(8,128)(2,1)S(1)}, s32[]{:T(128)}, /*index=5*/s32[]{:T(128)}) %tuple.81), condition=%wide.while_cond, body=%wide.while_body.sunk | while | flops 2 | bytes 27765 | solution.py:25
  98.4 2.3 reshape.278
  103.2 23.5 %while.20 = (s32[]{:T(128)}, f32[384,3797]{1,0:T(8,128)}, s32[8,2]{0,1:T(2,128)S(1)}, f32[8,1,3072]{2,1,0:T(1,128)S(1)}, s32[]{:T(128)}) while((s32[]{:T(128)}, f32[384,3797]{1,0:T(8,128)}, s32[8,2]{0,1:T(2,128)S(1)}, f32[8,1,3072]{2,1,0:T(1,128)S(1)}, s32[]{:T(128)}) %tuple.84), condition=%wide.while_cond.1, body=%wide.while_body.1.sunk | while | flops 2 | bytes 24685 | solution.py:26
  103.9 2.2 bitcast_dynamic-update-slice_fusion.2
  106.8 2.2 bitcast_dynamic-update-slice_fusion.2
  109.7 2.2 bitcast_dynamic-update-slice_fusion.2
  112.7 2.2 bitcast_dynamic-update-slice_fusion.2
  115.6 2.2 bitcast_dynamic-update-slice_fusion.2
  118.5 2.2 bitcast_dynamic-update-slice_fusion.2
  121.5 2.2 bitcast_dynamic-update-slice_fusion.2
  124.4 2.2 bitcast_dynamic-update-slice_fusion.2
  131.4 24.4 %while.19 = (s32[]{:T(128)}, bf16[384,4096]{1,0:T(8,128)(2,1)}, s32[8,2]{0,1:T(2,128)S(1)}, bf16[8,1,3456]{2,0,1:T(8,128)(2,1)S(1)}, s32[]{:T(128)}, /*index=5*/s32[]{:T(128)}) while((s32[]{:T(128)}, bf16[384,4096]{1,0:T(8,128)(2,1)}, s32[8,2]{0,1:T(2,128)S(1)}, bf16[8,1,3456]{2,0,1:T(8,128)(2,1)S(1)}, s32[]{:T(128)}, /*index=5*/s32[]{:T(128)}) %tuple.81), condition=%wide.while_cond, body=%wide.while_body.sunk | while | flops 2 | bytes 27765 | solution.py:25
  156.1 2.3 reshape.278
  160.9 23.5 %while.20 = (s32[]{:T(128)}, f32[384,3797]{1,0:T(8,128)}, s32[8,2]{0,1:T(2,128)S(1)}, f32[8,1,3072]{2,1,0:T(1,128)S(1)}, s32[]{:T(128)}) while((s32[]{:T(128)}, f32[384,3797]{1,0:T(8,128)}, s32[8,2]{0,1:T(2,128)S(1)}, f32[8,1,3072]{2,1,0:T(1,128)S(1)}, s32[]{:T(128)}) %tuple.84), condition=%wide.while_cond.1, body=%wide.while_body.1.sunk | while | flops 2 | bytes 24685 | solution.py:26
  164.5 2.2 bitcast_dynamic-update-slice_fusion.2
  167.4 2.2 bitcast_dynamic-update-slice_fusion.2
  170.4 2.2 bitcast_dynamic-update-slice_fusion.2
  173.3 2.2 bitcast_dynamic-update-slice_fusion.2
  176.2 2.2 bitcast_dynamic-update-slice_fusion.2
  179.2 2.2 bitcast_dynamic-update-slice_fusion.2
  182.1 2.2 bitcast_dynamic-update-slice_fusion.2
  189.1 24.4 %while.19 = (s32[]{:T(128)}, bf16[384,4096]{1,0:T(8,128)(2,1)}, s32[8,2]{0,1:T(2,128)S(1)}, bf16[8,1,3456]{2,0,1:T(8,128)(2,1)S(1)}, s32[]{:T(128)}, /*index=5*/s32[]{:T(128)}) while((s32[]{:T(128)}, bf16[384,4096]{1,0:T(8,128)(2,1)}, s32[8,2]{0,1:T(2,128)S(1)}, bf16[8,1,3456]{2,0,1:T(8,128)(2,1)S(1)}, s32[]{:T(128)}, /*index=5*/s32[]{:T(128)}) %tuple.81), condition=%wide.while_cond, body=%wide.while_body.sunk | while | flops 2 | bytes 27765 | solution.py:25
  213.9 2.3 reshape.278
  218.6 23.5 %while.20 = (s32[]{:T(128)}, f32[384,3797]{1,0:T(8,128)}, s32[8,2]{0,1:T(2,128)S(1)}, f32[8,1,3072]{2,1,0:T(1,128)S(1)}, s32[]{:T(128)}) while((s32[]{:T(128)}, f32[384,3797]{1,0:T(8,128)}, s32[8,2]{0,1:T(2,128)S(1)}, f32[8,1,3072]{2,1,0:T(1,128)S(1)}, s32[]{:T(128)}) %tuple.84), condition=%wide.while_cond.1, body=%wide.while_body.1.sunk | while | flops 2 | bytes 24685 | solution.py:26
  219.3 2.2 bitcast_dynamic-update-slice_fusion.2
  222.2 2.2 bitcast_dynamic-update-slice_fusion.2
  225.2 2.2 bitcast_dynamic-update-slice_fusion.2
  228.1 2.2 bitcast_dynamic-update-slice_fusion.2
  231.0 2.2 bitcast_dynamic-update-slice_fusion.2
  234.0 2.2 bitcast_dynamic-update-slice_fusion.2
  236.9 2.2 bitcast_dynamic-update-slice_fusion.2
  246.8 24.4 %while.19 = (s32[]{:T(128)}, bf16[384,4096]{1,0:T(8,128)(2,1)}, s32[8,2]{0,1:T(2,128)S(1)}, bf16[8,1,3456]{2,0,1:T(8,128)(2,1)S(1)}, s32[]{:T(128)}, /*index=5*/s32[]{:T(128)}) while((s32[]{:T(128)}, bf16[384,4096]{1,0:T(8,128)(2,1)}, s32[8,2]{0,1:T(2,128)S(1)}, bf16[8,1,3456]{2,0,1:T(8,128)(2,1)S(1)}, s32[]{:T(128)}, /*index=5*/s32[]{:T(128)}) %tuple.81), condition=%wide.while_cond, body=%wide.while_body.sunk | while | flops 2 | bytes 27765 | solution.py:25
  271.6 2.3 reshape.278
  276.3 23.5 %while.20 = (s32[]{:T(128)}, f32[384,3797]{1,0:T(8,128)}, s32[8,2]{0,1:T(2,128)S(1)}, f32[8,1,3072]{2,1,0:T(1,128)S(1)}, s32[]{:T(128)}) while((s32[]{:T(128)}, f32[384,3797]{1,0:T(8,128)}, s32[8,2]{0,1:T(2,128)S(1)}, f32[8,1,3072]{2,1,0:T(1,128)S(1)}, s32[]{:T(128)}) %tuple.84), condition=%wide.while_cond.1, body=%wide.while_body.1.sunk | while | flops 2 | bytes 24685 | solution.py:26
  277.0 2.2 bitcast_dynamic-update-slice_fusion.2
  279.9 2.2 bitcast_dynamic-update-slice_fusion.2
  282.9 2.2 bitcast_dynamic-update-slice_fusion.2
  285.8 2.2 bitcast_dynamic-update-slice_fusion.2
  288.7 2.2 bitcast_dynamic-update-slice_fusion.2
  291.7 2.2 bitcast_dynamic-update-slice_fusion.2
  304.5 24.4 %while.19 = (s32[]{:T(128)}, bf16[384,4096]{1,0:T(8,128)(2,1)}, s32[8,2]{0,1:T(2,128)S(1)}, bf16[8,1,3456]{2,0,1:T(8,128)(2,1)S(1)}, s32[]{:T(128)}, /*index=5*/s32[]{:T(128)}) while((s32[]{:T(128)}, bf16[384,4096]{1,0:T(8,128)(2,1)}, s32[8,2]{0,1:T(2,128)S(1)}, bf16[8,1,3456]{2,0,1:T(8,128)(2,1)S(1)}, s32[]{:T(128)}, /*index=5*/s32[]{:T(128)}) %tuple.81), condition=%wide.while_cond, body=%wide.while_body.sunk | while | flops 2 | bytes 27765 | solution.py:25
  329.3 2.3 reshape.278
  334.0 23.5 %while.20 = (s32[]{:T(128)}, f32[384,3797]{1,0:T(8,128)}, s32[8,2]{0,1:T(2,128)S(1)}, f32[8,1,3072]{2,1,0:T(1,128)S(1)}, s32[]{:T(128)}) while((s32[]{:T(128)}, f32[384,3797]{1,0:T(8,128)}, s32[8,2]{0,1:T(2,128)S(1)}, f32[8,1,3072]{2,1,0:T(1,128)S(1)}, s32[]{:T(128)}) %tuple.84), condition=%wide.while_cond.1, body=%wide.while_body.1.sunk | while | flops 2 | bytes 24685 | solution.py:26
  362.2 24.4 %while.19 = (s32[]{:T(128)}, bf16[384,4096]{1,0:T(8,128)(2,1)}, s32[8,2]{0,1:T(2,128)S(1)}, bf16[8,1,3456]{2,0,1:T(8,128)(2,1)S(1)}, s32[]{:T(128)}, /*index=5*/s32[]{:T(128)}) while((s32[]{:T(128)}, bf16[384,4096]{1,0:T(8,128)(2,1)}, s32[8,2]{0,1:T(2,128)S(1)}, bf16[8,1,3456]{2,0,1:T(8,128)(2,1)S(1)}, s32[]{:T(128)}, /*index=5*/s32[]{:T(128)}) %tuple.81), condition=%wide.while_cond, body=%wide.while_body.sunk | while | flops 2 | bytes 27765 | solution.py:25
  387.0 2.3 reshape.278
  391.7 23.5 %while.20 = (s32[]{:T(128)}, f32[384,3797]{1,0:T(8,128)}, s32[8,2]{0,1:T(2,128)S(1)}, f32[8,1,3072]{2,1,0:T(1,128)S(1)}, s32[]{:T(128)}) while((s32[]{:T(128)}, f32[384,3797]{1,0:T(8,128)}, s32[8,2]{0,1:T(2,128)S(1)}, f32[8,1,3072]{2,1,0:T(1,128)S(1)}, s32[]{:T(128)}) %tuple.84), condition=%wide.while_cond.1, body=%wide.while_body.1.sunk | while | flops 2 | bytes 24685 | solution.py:26
  419.9 24.4 %while.19 = (s32[]{:T(128)}, bf16[384,4096]{1,0:T(8,128)(2,1)}, s32[8,2]{0,1:T(2,128)S(1)}, bf16[8,1,3456]{2,0,1:T(8,128)(2,1)S(1)}, s32[]{:T(128)}, /*index=5*/s32[]{:T(128)}) while((s32[]{:T(128)}, bf16[384,4096]{1,0:T(8,128)(2,1)}, s32[8,2]{0,1:T(2,128)S(1)}, bf16[8,1,3456]{2,0,1:T(8,128)(2,1)S(1)}, s32[]{:T(128)}, /*index=5*/s32[]{:T(128)}) %tuple.81), condition=%wide.while_cond, body=%wide.while_body.sunk | while | flops 2 | bytes 27765 | solution.py:25
  444.7 2.3 reshape.278
  449.5 23.5 %while.20 = (s32[]{:T(128)}, f32[384,3797]{1,0:T(8,128)}, s32[8,2]{0,1:T(2,128)S(1)}, f32[8,1,3072]{2,1,0:T(1,128)S(1)}, s32[]{:T(128)}) while((s32[]{:T(128)}, f32[384,3797]{1,0:T(8,128)}, s32[8,2]{0,1:T(2,128)S(1)}, f32[8,1,3072]{2,1,0:T(1,128)S(1)}, s32[]{:T(128)}) %tuple.84), condition=%wide.while_cond.1, body=%wide.while_body.1.sunk | while | flops 2 | bytes 24685 | solution.py:26
  477.7 24.4 %while.19 = (s32[]{:T(128)}, bf16[384,4096]{1,0:T(8,128)(2,1)}, s32[8,2]{0,1:T(2,128)S(1)}, bf16[8,1,3456]{2,0,1:T(8,128)(2,1)S(1)}, s32[]{:T(128)}, /*index=5*/s32[]{:T(128)}) while((s32[]{:T(128)}, bf16[384,4096]{1,0:T(8,128)(2,1)}, s32[8,2]{0,1:T(2,128)S(1)}, bf16[8,1,3456]{2,0,1:T(8,128)(2,1)S(1)}, s32[]{:T(128)}, /*index=5*/s32[]{:T(128)}) %tuple.81), condition=%wide.while_cond, body=%wide.while_body.sunk | while | flops 2 | bytes 27765 | solution.py:25
  502.4 2.3 reshape.278
  507.2 23.5 %while.20 = (s32[]{:T(128)}, f32[384,3797]{1,0:T(8,128)}, s32[8,2]{0,1:T(2,128)S(1)}, f32[8,1,3072]{2,1,0:T(1,128)S(1)}, s32[]{:T(128)}) while((s32[]{:T(128)}, f32[384,3797]{1,0:T(8,128)}, s32[8,2]{0,1:T(2,128)S(1)}, f32[8,1,3072]{2,1,0:T(1,128)S(1)}, s32[]{:T(128)}) %tuple.84), condition=%wide.while_cond.1, body=%wide.while_body.1.sunk | while | flops 2 | bytes 24685 | solution.py:26
  533.4 11.2 %all_to_all.5 = f32[8,1,3072]{2,1,0:T(1,128)S(1)} all-to-all(f32[8,1,3072]{2,1,0:T(1,128)S(1)} %reshape.182), channel_id=1, replica_groups=mesh['span'=2,'tmpl'=2,'stn'=8] {'stn'}, dimensions={0} | all-to-all | bytes 196608 | tf_op jit(solution)/shard_map/all_to_all | solution.py:99
  (642 shorter events, 372.7 us)
Async XLA Ops:
  0.0 5.2 copy-start
  0.0 37.7 %collective-permute-start = (bf16[384,2048]{1,0:T(8,128)(2,1)}, bf16[384,2048]{1,0:T(8,128)(2,1)}, u32[]{:S(2)}, u32[]{:S(2)}) collective-permute-start(bf16[384,2048]{1,0:T(8,128)(2,1)} %param.7), channel_id=1, source_target_pairs={{0,8},{8,0},{1,9},{9,1},{2,10},{10,2},{3,11},{11,3},{4,12},{12,4},... | collective-permute-start | bytes 4718600 | tf_op jit(solution)/shard_map/ppermute | solution.py:52
  60.1 6.6 %copy-start.1 = (bf16[384,2048]{1,0:T(8,128)(2,1)S(1)}, bf16[384,2048]{1,0:T(8,128)(2,1)}, u32[]{:S(2)}) copy-start(bf16[384,2048]{1,0:T(8,128)(2,1)} %param.7) | copy-start | bytes 4718596
